TPU v7x, 256 devices: a whole 4x4x8 slice. The times are simulated.
256 devices in a mesh: lat: 32 (over z, y_hi, core), lon: 8 (over y_lo, x).
Axes of the slice: x: 4, y: 4 (y_hi: 2, y_lo: 2; y = y_hi * 2 + y_lo), z: 8, core: 2. Of those that a mesh axis runs over, the one named last changes fastest.
Arguments:
- state_field: bfloat16 [73, 256, 1024], P(None, 'lat', 'lon'), may hold values from -6 to 6
- support_rows: int32 [128, 5], P('lat'), may hold values from -2 to 2, as said below
- window_bands: int32 [32], replicated, may hold values from 0 to 127, as said below
- conv_weight: bfloat16 [5, 3, 73, 256], replicated, may hold values from -0.1875 to 0.1875
- w_query: bfloat16 [256, 256], replicated
- w_key: bfloat16 [256, 256], replicated
- w_value: bfloat16 [256, 256], replicated, may hold values from -0.375 to 0.375
- w_out: bfloat16 [256, 256], replicated, may hold values from -0.75 to 0.75
Outputs:
- window_out: bfloat16 [32, 512, 256], P('lat', 'lon')
Inputs may be any that keep to these rules, and one draw needn't show every extreme that they name: `support_rows`: each row is a permutation of the 5 offsets from -2 to 2. `window_bands`: 32 distinct token bands.
All inputs are finite; a program needn't handle non-finite values.
Results may differ from a plain program's by a relative error of at most 0.019.
Values may be sent and summed in bfloat16 or wider, within the bound.
A program may use at most 64 MiB of HBM per device.

v0:
```python
import math
import jax
import jax.numpy as jnp
from jax import lax
from jax.sharding import PartitionSpec as P

D = 256
H = 4


def padded(x, sides, width):
    for axis, dim in sides:
        devices, length = (lax.axis_size(axis), x.shape[dim])
        up = [(i, (i + 1) % devices) for i in range(devices - 1)]
        down = [(j, i) for i, j in up]
        last = lax.slice_in_dim(x, length - width, length, axis=dim)
        leading = lax.slice_in_dim(x, 0, width, axis=dim)
        before = lax.ppermute(last, axis, up)
        after = lax.ppermute(leading, axis, down)
        x = jnp.concatenate([before, x, after], axis=dim)
    return x


def shifted(x, axis, by):
    devices = lax.axis_size(axis)
    return lax.ppermute(x, axis, [(i, (i + by) % devices) for i in range(devices)])


def conv_features(extended, support_rows, conv_weight):
    bands = support_rows.shape[0]
    width = (extended.shape[2] - 1) // 2
    row_index = 2 * jnp.arange(bands, dtype=jnp.int32)[:, None] + support_rows + 2
    picked = jnp.take(extended, row_index, axis=1)
    tapped = jnp.stack(
        [picked[..., column_tap : column_tap + 2 * width : 2] for column_tap in range(3)], axis=3
    )
    patches = jnp.transpose(tapped, (1, 4, 2, 3, 0)).reshape(bands * width, -1)
    raw = jnp.dot(
        patches, conv_weight.reshape(-1, conv_weight.shape[-1]), preferred_element_type=jnp.float32
    )
    factor = lax.rsqrt(jnp.mean(raw * raw, axis=-1, keepdims=True) + 1e-06)
    return (raw * factor).astype(jnp.bfloat16).reshape(bands, width, -1)


def absorb(carry, block_keys, block_values, block_area, queries, scale):
    running_max, running_sum, mixed = carry
    scores = (
        jnp.einsum("qhd,khd->qhk", queries, block_keys, preferred_element_type=jnp.float32) * scale
        + block_area
    )
    new_max = jnp.maximum(running_max, jnp.max(scores, axis=-1))
    factor = jnp.exp(running_max - new_max)
    weights = jnp.exp(scores - new_max[..., None])
    running_sum = running_sum * factor + jnp.sum(weights, axis=-1)
    update = jnp.einsum(
        "qhk,khd->qhd",
        weights.astype(jnp.bfloat16),
        block_values,
        preferred_element_type=jnp.float32,
    )
    mixed = mixed * factor[..., None] + update
    return (new_max, running_sum, mixed)


def sweep(carry, keys, values, queries, band_total):
    rows = keys.shape[0]
    lon_tile = keys.shape[1]
    head_size = D // H
    band_block = math.gcd(rows, max(1, 512 // lon_tile))
    blocks = rows // band_block
    block_len = band_block * lon_tile
    keys_blocks = keys.reshape(blocks, block_len, H, head_size)
    values_blocks = values.reshape(blocks, block_len, H, head_size)
    band_index = jnp.arange(rows, dtype=jnp.int32).astype(jnp.float32)
    centre = (band_index + 0.5) * (math.pi / band_total) - math.pi / 2
    area_rows = jnp.repeat(jnp.log(jnp.cos(centre)), lon_tile).reshape(blocks, block_len)
    scale = 1.0 / math.sqrt(head_size)

    def step_block(state, inputs):
        return (absorb(state, inputs[0], inputs[1], inputs[2], queries, scale), None)

    result, unused = lax.scan(step_block, carry, (keys_blocks, values_blocks, area_rows))
    return result


def per_device(
    state_field, support_rows, window_bands, conv_weight, w_query, w_key, w_value, w_out
):
    lat_tile = support_rows.shape[0]
    lon_tile = state_field.shape[2] // 2
    whole_lon = lon_tile * lax.axis_size("lon")
    band_total = lat_tile * lax.axis_size("lat")
    head_size = D // H
    extended = padded(state_field, (("lat", 1),), 2)
    western = shifted(extended[:, :, -1:], "lon", 1)
    extended = jnp.concatenate([western, extended], axis=2)
    features = conv_features(extended, support_rows, conv_weight)
    flat = features.reshape(-1, D)
    slot_count = window_bands.shape[0] // lax.axis_size("lat")
    local_queries = jnp.dot(flat, w_query, preferred_element_type=jnp.float32).astype(jnp.bfloat16)
    local_queries = local_queries.reshape(lat_tile, lon_tile * D)
    first_band = lax.axis_index("lat") * lat_tile
    wanted = window_bands - first_band
    onehot = (wanted[:, None] == jnp.arange(lat_tile, dtype=jnp.int32)[None, :]).astype(
        jnp.bfloat16
    )
    picked = jnp.dot(onehot, local_queries, preferred_element_type=jnp.float32)
    picked = picked.astype(jnp.bfloat16).astype(jnp.float32)
    mine = lax.psum_scatter(
        picked.reshape(slot_count * lax.axis_size("lat"), lon_tile, D).astype(jnp.bfloat16),
        "lat",
        scatter_dimension=0,
        tiled=True,
    )
    gathered = lax.all_gather(mine, "lon", axis=1, tiled=True)
    query_count = slot_count * whole_lon
    queries = gathered.reshape(query_count, H, head_size)
    initial = (
        jnp.full((query_count, H), -1e30, jnp.float32),
        jnp.zeros((query_count, H), jnp.float32),
        jnp.zeros((query_count, H, head_size), jnp.float32),
    )
    keys_local = (
        jnp.dot(flat, w_key, preferred_element_type=jnp.float32)
        .astype(jnp.bfloat16)
        .reshape(lat_tile, lon_tile, D)
    )
    values_local = (
        jnp.dot(flat, w_value, preferred_element_type=jnp.float32)
        .astype(jnp.bfloat16)
        .reshape(lat_tile, lon_tile, D)
    )
    carry = sweep(
        initial,
        lax.all_gather(keys_local, "lat", axis=0, tiled=True),
        lax.all_gather(values_local, "lat", axis=0, tiled=True),
        queries,
        band_total,
    )
    running_max, running_sum, mixed = carry
    best = lax.pmax(running_max, "lon")
    factor = jnp.exp(running_max - best)
    scaled_mix = (mixed * factor[..., None]).reshape(slot_count, whole_lon, D)
    scaled_sum = (running_sum * factor).reshape(slot_count, whole_lon, H)
    mix_share, sum_share = (
        lax.psum_scatter(
            scaled_mix.astype(jnp.bfloat16), "lon", scatter_dimension=1, tiled=True
        ).astype(jnp.float32),
        lax.psum_scatter(
            scaled_sum.astype(jnp.bfloat16), "lon", scatter_dimension=1, tiled=True
        ).astype(jnp.float32),
    )
    attended = mix_share.reshape(slot_count, lon_tile, H, head_size) / sum_share[..., None]
    attended = attended.astype(jnp.bfloat16).reshape(slot_count * lon_tile, D)
    result = jnp.dot(attended, w_out, preferred_element_type=jnp.float32).astype(jnp.bfloat16)
    return result.reshape(slot_count, lon_tile, D)


def solution(mesh):
    return jax.shard_map(
        per_device,
        mesh=mesh,
        in_specs=(P(None, "lat", "lon"), P("lat", None), P(), P(), P(), P(), P(), P()),
        out_specs=P("lat", "lon", None),
        check_vma=False,
    )
```

profile of v0, /device:TPU:32, one launch (start us, length us, event | category | flops | bytes accessed | tf_op | source)
XLA Modules:
  0.0 605.1 jit_solution(1551652999318973012)
XLA Ops:
  7.7 1.9 collective-permute-start
  9.7 6.0 collective-permute-start.1
  20.4 3.0 collective-permute-done.2
  26.8 1.8 slice.23
  35.6 114.5 %reduce-scatter.8.cloned.1.call-done = bf16[1,64,256]{2,1,0:T(8,128)(2,1)} async-done(((bf16[32,64,256]{2,1,0:T(8,128)(2,1)}), bf16[1,64,256]{2,1,0:T(8,128)(2,1)}) %reduce-scatter.8.cloned.1.call-update) | async-done | bytes 32784 | tf_op jit(solution)/shard_map/reduce_scatter | solution.py:109
  150.1 28.8 %all_gather.10 = bf16[1,512,256]{2,1,0:T(8,128)(2,1)S(1)} all-gather(bf16[1,64,256]{2,1,0:T(8,128)(2,1)} %reduce-scatter.8.cloned.1.call-done), channel_id=1, replica_groups=mesh['lat'=32,'lon'=8] {'lon'}, dimensions={1}, use_global_device_ids=true | all-gather | bytes 294912 | tf_op jit(solution)/shard_map/all_gather | solution.py:115
  179.0 59.0 %all-gather.3.cloned.1.call-done = bf16[128,64,256]{2,1,0:T(8,128)(2,1)} async-done(((bf16[4,64,256]{2,1,0:T(8,128)(2,1)}), bf16[128,64,256]{2,1,0:T(8,128)(2,1)}) %all-gather.3.cloned.1.call-update) | async-done | bytes 4194320 | tf_op jit(solution)/shard_map/all_gather | solution.py:135
  238.1 12.9 %reshape.113 = bf16[16,512,4,64]{3,2,1,0:T(4,128)(2,1)} reshape(bf16[128,64,256]{2,1,0:T(8,128)(2,1)} %all-gather.3.cloned.1.call-done) | data formatting | bytes 8388608 | tf_op jit(solution)/shard_map/reshape | solution.py:72
  251.0 12.7 %copy.29 = bf16[16,512,4,64]{1,3,2,0:T(8,128)(2,1)} copy(bf16[16,512,4,64]{3,2,1,0:T(4,128)(2,1)} %reshape.113) | data formatting | bytes 8388608
  263.7 60.5 %all-gather.5.cloned.1.call-done = bf16[128,64,256]{2,1,0:T(8,128)(2,1)} async-done(((bf16[4,64,256]{2,1,0:T(8,128)(2,1)}), bf16[128,64,256]{2,1,0:T(8,128)(2,1)}) %all-gather.5.cloned.1.call-update) | async-done | bytes 4194320 | tf_op jit(solution)/shard_map/all_gather | solution.py:136
  324.2 12.9 %reshape.114 = bf16[16,512,4,64]{3,2,1,0:T(4,128)(2,1)} reshape(bf16[128,64,256]{2,1,0:T(8,128)(2,1)} %all-gather.5.cloned.1.call-done) | data formatting | bytes 8388608 | tf_op jit(solution)/shard_map/reshape | solution.py:73
  337.1 12.7 %copy.30 = bf16[16,512,4,64]{1,3,2,0:T(8,128)(2,1)} copy(bf16[16,512,4,64]{3,2,1,0:T(4,128)(2,1)} %reshape.114) | data formatting | bytes 8388608
  349.8 150.0 %while.15 = (s32[]{:T(128)}, f32[512,4]{0,1:T(4,128)S(1)}, f32[512,4]{0,1:T(4,128)S(1)}, f32[512,4,64]{0,2,1:T(8,128)S(1)}, bf16[16,512,4,64]{1,3,2,0:T(8,128)(2...) while((s32[]{:T(128)}, f32[512,4]{0,1:T(4,128)S(1)}, ...), condition=%wide.region_5.6_spmd.clone, body=%wide.region_2.0_spmd.clone.sunk | while | flops 280373248 | bytes 31337616 | solution.py:82
  349.8 3.8 bitcast_reduce_fusion.2
  353.6 3.2 fusion.46
  357.1 2.1 fusion.48
  359.2 3.8 bitcast_reduce_fusion.2
  363.0 3.2 fusion.46
  366.5 2.1 fusion.48
  368.6 3.8 bitcast_reduce_fusion.2
  372.4 3.2 fusion.46
  375.8 2.1 fusion.48
  378.0 3.8 bitcast_reduce_fusion.2
  381.8 3.2 fusion.46
  385.2 2.1 fusion.48
  387.3 3.8 bitcast_reduce_fusion.2
  391.1 3.2 fusion.46
  394.6 2.1 fusion.48
  396.7 3.8 bitcast_reduce_fusion.2
  400.5 3.2 fusion.46
  404.0 2.1 fusion.48
  406.1 3.8 bitcast_reduce_fusion.2
  409.9 3.2 fusion.46
  413.3 2.1 fusion.48
  415.5 3.8 bitcast_reduce_fusion.2
  419.3 3.2 fusion.46
  422.7 2.1 fusion.48
  424.8 3.8 bitcast_reduce_fusion.2
  428.6 3.2 fusion.46
  432.1 2.1 fusion.48
  434.2 3.8 bitcast_reduce_fusion.2
  438.0 3.2 fusion.46
  441.4 2.1 fusion.48
  443.6 3.8 bitcast_reduce_fusion.2
  447.4 3.2 fusion.46
  450.8 2.1 fusion.48
  452.9 3.8 bitcast_reduce_fusion.2
  456.8 3.2 fusion.46
  460.2 2.1 fusion.48
  462.3 3.8 bitcast_reduce_fusion.2
  466.1 3.2 fusion.46
  469.6 2.1 fusion.48
  471.7 3.8 bitcast_reduce_fusion.2
  475.5 3.2 fusion.46
  478.9 2.1 fusion.48
  481.1 3.8 bitcast_reduce_fusion.2
  484.9 3.2 fusion.46
  488.3 2.1 fusion.48
  490.4 3.8 bitcast_reduce_fusion.2
  494.2 3.2 fusion.46
  497.7 2.1 fusion.48
  499.8 18.9 %pmax.7 = f32[512,4]{0,1:T(4,128)S(1)} all-reduce(f32[512,4]{0,1:T(4,128)S(1)} %get-tuple-element.50), channel_id=1, replica_groups=mesh['lat'=32,'lon'=8] {'lon'}, use_global_device_ids=true, to_apply=%region_6.7 | all-reduce | flops 2048 | bytes 16384 | tf_op jit(solution)/shard_map/pmax | solution.py:141
  520.9 34.4 %reduce-scatter.12.cloned.1.call-done = bf16[64,4]{1,0:T(8,128)(2,1)} async-done(((bf16[512,4]{1,0:T(8,128)(2,1)}), bf16[64,4]{1,0:T(8,128)(2,1)}) %reduce-scatter.12.cloned.1.call-update) | async-done | bytes 528
  556.2 40.6 %reduce-scatter.10.cloned.1.call-done = bf16[64,256]{1,0:T(8,128)(2,1)} async-done(((bf16[512,256]{1,0:T(8,128)(2,1)}), bf16[64,256]{1,0:T(8,128)(2,1)}) %reduce-scatter.10.cloned.1.call-update) | async-done | bytes 32784
  (163 shorter events, 24.4 us)
Async XLA Ops:
  6.5 24.8 %copy-start = (bf16[256,256]{1,0:T(8,128)(2,1)S(1)}, bf16[256,256]{1,0:T(8,128)(2,1)}, u32[]{:S(2)}) copy-start(bf16[256,256]{1,0:T(8,128)(2,1)} %param.14) | copy-start | bytes 393220
  6.5 143.6 %reduce-scatter.8.cloned.1.call-start = ((), (), s32[]{:S(2)}) async-start(), calls=%async_computation.4 | async-start | bytes 1081344 | tf_op jit(solution)/shard_map/reduce_scatter | solution.py:109
  7.7 9.5 %collective-permute-start = (bf16[73,2,128]{0,2,1:T(8,128)(2,1)S(1)}, bf16[73,2,128]{0,2,1:T(8,128)(2,1)S(1)}, u32[]{:S(2)}, u32[]{:S(2)}) collective-permute-start(bf16[73,2,128]{0,2,1:T(8,128)(2,1)S(1)} %get-tuple-element.119), channel_id=1, source_target_pairs={{0,8},{8,16},{16,24},{24,32},{32,40},{40,48},{48,56},{56,64},{64,7... | collective-permute-start | bytes 112136 | tf_op jit(solution)/shard_map/ppermute | solution.py:18
  9.7 7.9 %collective-permute-start.1 = (bf16[73,2,128]{0,2,1:T(8,128)(2,1)S(1)}, bf16[73,2,128]{0,2,1:T(8,128)(2,1)S(1)}, u32[]{:S(2)}, u32[]{:S(2)}) collective-permute-start(bf16[73,2,128]{0,2,1:T(8,128)(2,1)S(1)} %get-tuple-element.120), channel_id=1, source_target_pairs={{8,0},{16,8},{24,16},{32,24},{40,32},{48,40},{56,48},{64,56},{72,6... | collective-permute-start | bytes 112136 | tf_op jit(solution)/shard_map/ppermute | solution.py:19
  17.6 5.8 collective-permute-start.2
  29.7 3.7 copy-start.2
  29.8 4.7 copy-start.3
  33.4 204.7 %all-gather.3.cloned.1.call-start = ((), (), s32[]{:S(2)}) async-start(), calls=%async_computation.3 | async-start | bytes 4325376 | tf_op jit(solution)/shard_map/all_gather | solution.py:135
  34.4 289.8 %all-gather.5.cloned.1.call-start = ((), (), s32[]{:S(2)}) async-start(), calls=%async_computation.5 | async-start | bytes 4325376 | tf_op jit(solution)/shard_map/all_gather | solution.py:136
  35.3 520.0 %reduce-scatter.12.cloned.1.call-start = ((), (), s32[]{:S(2)}) async-start(), calls=%async_computation.7 | async-start | bytes 147456
  349.8 247.9 %copy-start.4 = (bf16[256,256]{1,0:T(8,128)(2,1)S(1)}, bf16[256,256]{1,0:T(8,128)(2,1)}, u32[]{:S(2)}) copy-start(bf16[256,256]{1,0:T(8,128)(2,1)} %param.17) | copy-start | bytes 393220
  353.6 3.4 copy-start.1
  363.0 3.4 copy-start.1
  372.4 3.4 copy-start.1
  381.8 3.4 copy-start.1
  391.1 3.4 copy-start.1
  400.5 3.4 copy-start.1
  409.9 3.4 copy-start.1
  419.3 3.4 copy-start.1
  428.6 3.4 copy-start.1
  438.0 3.4 copy-start.1
  447.4 3.4 copy-start.1
  456.7 3.4 copy-start.1
  466.1 3.4 copy-start.1
  475.5 3.4 copy-start.1
  484.9 3.4 copy-start.1
  494.2 3.4 copy-start.1
  519.6 77.1 %reduce-scatter.10.cloned.1.call-start = ((), (), s32[]{:S(2)}) async-start(), calls=%async_computation.6 | async-start | bytes 294912
Sparse Core Ops, SparseCore 0:
  33.5 116.5 reduce-scatter.7
  152.9 85.1 all-gather.2
  240.9 83.2 all-gather.4
  519.7 35.5 reduce-scatter.11
  557.7 39.0 reduce-scatter.9
where the time goes:
time: 608 us; the launch traced here: 605 us
  waiting for transfers between devices  312 us (51%)
  matrix products  97.6 us (16%)
  local copies, waits for them, and re-layouts  69 us (11%)
  other arithmetic  54.4 us (9%)
  blocking collectives  47.7 us (8%)
  between operations  13.4 us (2%)
  starting transfers between devices  9.7 us (2%)
    reduce_scatter x1, waiting for transfers between devices, per_device(): lax.psum_scatter(picked.reshape(slot_count * lax.axis_size('lat'), lon_ti...  114 us
    unnamed x7, waiting for transfers between devices  75.1 us
    dot_general x16, matrix products, absorb(): jnp.einsum('qhd,khd->qhk', queries, block_keys, preferred_element_type=jn...  60.8 us
    all_gather x1, waiting for transfers between devices, per_device(): lax.all_gather(values_local, 'lat', axis=0, tiled=True)  60.5 us
    all_gather x1, waiting for transfers between devices, per_device(): lax.all_gather(keys_local, 'lat', axis=0, tiled=True)  59 us
    reduce_sum x16, other arithmetic, absorb(): running_sum = running_sum * factor + jnp.sum(weights, axis=-1)  51.8 us
    dot_general x16, matrix products, absorb(): jnp.einsum('qhk,khd->qhd', weights.astype(jnp.bfloat16), block_values, pr...  33.2 us
    unnamed x20, local copies, waits for them, and re-layouts  31.6 us
  transfers between devices with their start and end apart: 8, of which 7 were waited for; matrix products, arithmetic and copies ran while one was open for 5% of the time, Pallas kernels for 0%

commit v1 on v0

--- a/solution.py
+++ b/solution.py
@@ -6,6 +6,13 @@
 
 D = 256
 H = 4
+
+
+def exchange_gather(value, mesh_axis, dim):
+    size = lax.axis_size(mesh_axis)
+    blocks = jnp.stack([value for _ in range(size)])
+    blocks = lax.all_to_all(blocks, mesh_axis, split_axis=0, concat_axis=0)
+    return jnp.concatenate(blocks, axis=dim)
 
 
 def padded(x, sides, width):
@@ -132,7 +139,7 @@
     )
     carry = sweep(
         initial,
-        lax.all_gather(keys_local, "lat", axis=0, tiled=True),
+        exchange_gather(keys_local, "lat", 0),
         lax.all_gather(values_local, "lat", axis=0, tiled=True),
         queries,
         band_total,

time: 608 us -> 532 us (0.88)
  waiting for transfers between devices: 312 us -> 223 us
  starting transfers between devices: 9.7 us -> 21.9 us
    all_gather x1 -> x0, waiting for transfers between devices: 59 us -> none  [per_device(): lax.all_gather(keys_local, 'lat', axis=0, tiled=True)]
    all_gather x1, waiting for transfers between devices: 60.5 us -> 32.8 us  [per_device(): lax.all_gather(values_local, 'lat', axis=0, tiled=True)]
    another operation x0 -> x2, local copies, waits for them, and re-layouts: none -> 15.4 us  [the longest x1 13 us: sweep(): keys_blocks = keys.reshape(blocks, block_len, H, head_size)]
    reshape x1 -> x0, local copies, waits for them, and re-layouts: 12.9 us -> none  [sweep(): keys_blocks = keys.reshape(blocks, block_len, H, head_size)]
    all_to_all x0 -> x1, starting transfers between devices: none -> 12.2 us  [exchange_gather(): blocks = lax.all_to_all(blocks, mesh_axis, split_axis=0, concat_axis=0)]
    unnamed x7 -> x6, waiting for transfers between devices: 75.1 us -> 75.1 us
  transfers between devices with their start and end apart: 8 -> 8, of which waited for: 7 -> 6; matrix products, arithmetic and copies ran while one was open for 5% -> 6% of each run, Pallas kernels for 0% -> 0%
where the time goes in v1:
time: 532 us; the launch traced here: 530 us
  waiting for transfers between devices  223 us (42%)
  matrix products  96.8 us (18%)
  local copies, waits for them, and re-layouts  71.5 us (13%)
  other arithmetic  54.4 us (10%)
  blocking collectives  47.8 us (9%)
  starting transfers between devices  21.9 us (4%)
  between operations  13.4 us (3%)
    reduce_scatter x1, waiting for transfers between devices, per_device(): lax.psum_scatter(picked.reshape(slot_count * lax.axis_size('lat'), lon_ti...  112 us
    unnamed x6, waiting for transfers between devices  75.1 us
    dot_general x16, matrix products, absorb(): jnp.einsum('qhd,khd->qhk', queries, block_keys, preferred_element_type=jn...  60.6 us
    reduce_sum x16, other arithmetic, absorb(): running_sum = running_sum * factor + jnp.sum(weights, axis=-1)  51.8 us
    dot_general x16, matrix products, absorb(): jnp.einsum('qhk,khd->qhd', weights.astype(jnp.bfloat16), block_values, pr...  33.2 us
    all_gather x1, waiting for transfers between devices, per_device(): lax.all_gather(values_local, 'lat', axis=0, tiled=True)  32.8 us
    unnamed x20, local copies, waits for them, and re-layouts  31.6 us
    all_gather x1, blocking collectives, per_device(): gathered = lax.all_gather(mine, 'lon', axis=1, tiled=True)  28.9 us
  transfers between devices with their start and end apart: 8, of which 6 were waited for; matrix products, arithmetic and copies ran while one was open for 6% of the time, Pallas kernels for 0%

profile of v1, /device:TPU:32, one launch (start us, length us, event | category | flops | bytes accessed | tf_op | source)
XLA Modules:
  0.0 529.9 jit_solution(8567680295670568571)
XLA Ops:
  7.7 1.9 collective-permute-start
  9.7 6.0 %collective-permute-start.1 = (bf16[73,2,128]{0,2,1:T(8,128)(2,1)S(1)}, bf16[73,2,128]{0,2,1:T(8,128)(2,1)S(1)}, u32[]{:S(2)}, u32[]{:S(2)}) collective-permute-start(bf16[73,2,128]{0,2,1:T(8,128)(2,1)S(1)} %get-tuple-element.120), channel_id=1, source_target_pairs={{8,0},{16,8},{24,16},{32,24},{40,32},{48,40},{56,48},{64,56},{72,6... | collective-permute-start | bytes 112136 | tf_op jit(solution)/shard_map/ppermute | solution.py:26
  20.4 3.0 collective-permute-done.2
  33.6 2.5 stack.19
  36.1 12.2 %all-to-all-start = ((bf16[32,4,64,256]{3,2,1,0:T(8,128)(2,1)}), bf16[32,4,64,256]{3,2,1,0:T(8,128)(2,1)}, u32[]{:S(2)}, u32[]{:S(2)}) async-start(bf16[32,4,64,256]{3,2,1,0:T(8,128)(2,1)} %stack.19), calls=%async_computation | async-start | bytes 8388608 | tf_op jit(solution)/shard_map/all_to_all | solution.py:14
  49.6 112.0 %reduce-scatter.8.cloned.1.call-done = bf16[1,64,256]{2,1,0:T(8,128)(2,1)} async-done(((bf16[32,64,256]{2,1,0:T(8,128)(2,1)}), bf16[1,64,256]{2,1,0:T(8,128)(2,1)}) %reduce-scatter.8.cloned.1.call-update) | async-done | bytes 32784 | tf_op jit(solution)/shard_map/reduce_scatter | solution.py:116
  161.6 28.9 %all_gather.6 = bf16[1,512,256]{2,1,0:T(8,128)(2,1)S(1)} all-gather(bf16[1,64,256]{2,1,0:T(8,128)(2,1)} %reduce-scatter.8.cloned.1.call-done), channel_id=1, replica_groups=mesh['lat'=32,'lon'=8] {'lon'}, dimensions={1}, use_global_device_ids=true | all-gather | bytes 294912 | tf_op jit(solution)/shard_map/all_gather | solution.py:122
  190.7 13.0 %reshape_reshape.4 = bf16[16,512,4,64]{3,2,1,0:T(4,128)(2,1)} reshape(bf16[32,4,64,256]{3,2,1,0:T(8,128)(2,1)} %all-to-all-done) | data formatting | bytes 8388608 | tf_op jit(solution)/shard_map/reshape;reshape | solution.py:79
  203.6 12.7 %copy.27 = bf16[16,512,4,64]{1,3,2,0:T(8,128)(2,1)} copy(bf16[16,512,4,64]{3,2,1,0:T(4,128)(2,1)} %reshape_reshape.4) | data formatting | bytes 8388608
  216.4 32.8 %all-gather.2.cloned.1.call-done = bf16[128,64,256]{2,1,0:T(8,128)(2,1)} async-done(((bf16[4,64,256]{2,1,0:T(8,128)(2,1)}), bf16[128,64,256]{2,1,0:T(8,128)(2,1)}) %all-gather.2.cloned.1.call-update) | async-done | bytes 4194320 | tf_op jit(solution)/shard_map/all_gather | solution.py:143
  249.2 12.9 %reshape.107 = bf16[16,512,4,64]{3,2,1,0:T(4,128)(2,1)} reshape(bf16[128,64,256]{2,1,0:T(8,128)(2,1)} %all-gather.2.cloned.1.call-done) | data formatting | bytes 8388608 | tf_op jit(solution)/shard_map/reshape | solution.py:80
  262.1 12.7 %copy.28 = bf16[16,512,4,64]{1,3,2,0:T(8,128)(2,1)} copy(bf16[16,512,4,64]{3,2,1,0:T(4,128)(2,1)} %reshape.107) | data formatting | bytes 8388608
  274.9 149.8 %while.15 = (s32[]{:T(128)}, f32[512,4]{0,1:T(4,128)S(1)}, f32[512,4]{0,1:T(4,128)S(1)}, f32[512,4,64]{0,2,1:T(8,128)S(1)}, bf16[16,512,4,64]{1,3,2,0:T(8,128)(2...) while((s32[]{:T(128)}, f32[512,4]{0,1:T(4,128)S(1)}, ...), condition=%wide.region_5.6_spmd.clone, body=%wide.region_2.0_spmd.clone.sunk | while | flops 280373248 | bytes 31337616 | solution.py:89
  274.9 3.8 bitcast_reduce_fusion.2
  278.7 3.2 fusion.46
  282.1 2.1 fusion.48
  284.3 3.8 bitcast_reduce_fusion.2
  288.1 3.2 fusion.46
  291.5 2.1 fusion.48
  293.6 3.8 bitcast_reduce_fusion.2
  297.4 3.2 fusion.46
  300.9 2.1 fusion.48
  303.0 3.8 bitcast_reduce_fusion.2
  306.8 3.2 fusion.46
  310.2 2.1 fusion.48
  312.3 3.8 bitcast_reduce_fusion.2
  316.1 3.2 fusion.46
  319.6 2.1 fusion.48
  321.7 3.8 bitcast_reduce_fusion.2
  325.5 3.2 fusion.46
  328.9 2.1 fusion.48
  331.1 3.8 bitcast_reduce_fusion.2
  334.9 3.2 fusion.46
  338.3 2.1 fusion.48
  340.4 3.8 bitcast_reduce_fusion.2
  344.2 3.2 fusion.46
  347.7 2.1 fusion.48
  349.8 3.8 bitcast_reduce_fusion.2
  353.6 3.2 fusion.46
  357.0 2.1 fusion.48
  359.1 3.8 bitcast_reduce_fusion.2
  362.9 3.2 fusion.46
  366.4 2.1 fusion.48
  368.5 3.8 bitcast_reduce_fusion.2
  372.3 3.2 fusion.46
  375.7 2.1 fusion.48
  377.9 3.8 bitcast_reduce_fusion.2
  381.7 3.2 fusion.46
  385.1 2.1 fusion.48
  387.2 3.8 bitcast_reduce_fusion.2
  391.0 3.2 fusion.46
  394.5 2.1 fusion.48
  396.6 3.8 bitcast_reduce_fusion.2
  400.4 3.2 fusion.46
  403.8 2.1 fusion.48
  405.9 3.8 bitcast_reduce_fusion.2
  409.7 3.2 fusion.46
  413.2 2.1 fusion.48
  415.3 3.8 bitcast_reduce_fusion.2
  419.1 3.2 fusion.46
  422.5 2.1 fusion.48
  424.6 18.9 %pmax.7 = f32[512,4]{0,1:T(4,128)S(1)} all-reduce(f32[512,4]{0,1:T(4,128)S(1)} %get-tuple-element.50), channel_id=1, replica_groups=mesh['lat'=32,'lon'=8] {'lon'}, use_global_device_ids=true, to_apply=%region_6.7 | all-reduce | flops 2048 | bytes 16384 | tf_op jit(solution)/shard_map/pmax | solution.py:148
  445.8 34.4 %reduce-scatter.12.cloned.1.call-done = bf16[64,4]{1,0:T(8,128)(2,1)} async-done(((bf16[512,4]{1,0:T(8,128)(2,1)}), bf16[64,4]{1,0:T(8,128)(2,1)}) %reduce-scatter.12.cloned.1.call-update) | async-done | bytes 528
  481.0 40.6 %reduce-scatter.10.cloned.1.call-done = bf16[64,256]{1,0:T(8,128)(2,1)} async-done(((bf16[512,256]{1,0:T(8,128)(2,1)}), bf16[64,256]{1,0:T(8,128)(2,1)}) %reduce-scatter.10.cloned.1.call-update) | async-done | bytes 32784
  (163 shorter events, 25.4 us)
Async XLA Ops:
  6.5 24.8 %copy-start = (bf16[256,256]{1,0:T(8,128)(2,1)S(1)}, bf16[256,256]{1,0:T(8,128)(2,1)}, u32[]{:S(2)}) copy-start(bf16[256,256]{1,0:T(8,128)(2,1)} %param.14) | copy-start | bytes 393220
  6.5 155.1 %reduce-scatter.8.cloned.1.call-start = ((), (), s32[]{:S(2)}) async-start(), calls=%async_computation.4 | async-start | bytes 1081344 | tf_op jit(solution)/shard_map/reduce_scatter | solution.py:116
  7.7 9.5 %collective-permute-start = (bf16[73,2,128]{0,2,1:T(8,128)(2,1)S(1)}, bf16[73,2,128]{0,2,1:T(8,128)(2,1)S(1)}, u32[]{:S(2)}, u32[]{:S(2)}) collective-permute-start(bf16[73,2,128]{0,2,1:T(8,128)(2,1)S(1)} %get-tuple-element.119), channel_id=1, source_target_pairs={{0,8},{8,16},{16,24},{24,32},{32,40},{40,48},{48,56},{56,64},{64,7... | collective-permute-start | bytes 112136 | tf_op jit(solution)/shard_map/ppermute | solution.py:25
  9.7 7.9 %collective-permute-start.1 = (bf16[73,2,128]{0,2,1:T(8,128)(2,1)S(1)}, bf16[73,2,128]{0,2,1:T(8,128)(2,1)S(1)}, u32[]{:S(2)}, u32[]{:S(2)}) collective-permute-start(bf16[73,2,128]{0,2,1:T(8,128)(2,1)S(1)} %get-tuple-element.120), channel_id=1, source_target_pairs={{8,0},{16,8},{24,16},{32,24},{40,32},{48,40},{56,48},{64,56},{72,6... | collective-permute-start | bytes 112136 | tf_op jit(solution)/shard_map/ppermute | solution.py:26
  17.6 5.8 %collective-permute-start.2 = (bf16[73,12,1]{0,2,1:T(2,128)(2,1)S(1)}, bf16[73,12,1]{0,2,1:T(2,128)(2,1)S(1)}, u32[]{:S(2)}, u32[]{:S(2)}) collective-permute-start(bf16[73,12,1]{0,2,1:T(2,128)(2,1)S(1)} %pad_maximum_fusion), channel_id=1, source_target_pairs={{0,1},{1,2},{2,3},{3,4},{4,5},{5,6},{6,7},{7,0},{8,9},{9,10},{10,1... | collective-permute-start | bytes 5264 | tf_op jit(solution)/shard_map/ppermute | solution.py:33
  29.7 3.6 copy-start.2
  36.1 12.3 %copy-start.3 = (bf16[256,256]{1,0:T(8,128)(2,1)S(1)}, bf16[256,256]{1,0:T(8,128)(2,1)}, u32[]{:S(2)}) copy-start(bf16[256,256]{1,0:T(8,128)(2,1)} %param.16) | copy-start | bytes 393220
  36.1 154.6 %all-to-all-start = ((bf16[32,4,64,256]{3,2,1,0:T(8,128)(2,1)}), bf16[32,4,64,256]{3,2,1,0:T(8,128)(2,1)}, u32[]{:S(2)}, u32[]{:S(2)}) async-start(bf16[32,4,64,256]{3,2,1,0:T(8,128)(2,1)} %stack.19), calls=%async_computation | async-start | bytes 8388608 | tf_op jit(solution)/shard_map/all_to_all | solution.py:14
  48.3 200.9 %all-gather.2.cloned.1.call-start = ((), (), s32[]{:S(2)}) async-start(), calls=%async_computation.5 | async-start | bytes 4325376 | tf_op jit(solution)/shard_map/all_gather | solution.py:143
  49.3 430.9 %reduce-scatter.12.cloned.1.call-start = ((), (), s32[]{:S(2)}) async-start(), calls=%async_computation.7 | async-start | bytes 147456
  274.9 247.7 %copy-start.4 = (bf16[256,256]{1,0:T(8,128)(2,1)S(1)}, bf16[256,256]{1,0:T(8,128)(2,1)}, u32[]{:S(2)}) copy-start(bf16[256,256]{1,0:T(8,128)(2,1)} %param.17) | copy-start | bytes 393220
  278.7 3.4 copy-start.1
  288.0 3.4 copy-start.1
  297.4 3.4 copy-start.1
  306.8 3.4 copy-start.1
  316.1 3.4 copy-start.1
  325.5 3.4 copy-start.1
  334.8 3.4 copy-start.1
  344.2 3.4 copy-start.1
  353.6 3.4 copy-start.1
  362.9 3.4 copy-start.1
  372.3 3.4 copy-start.1
  381.7 3.4 copy-start.1
  391.0 3.4 copy-start.1
  400.4 3.4 copy-start.1
  409.7 3.4 copy-start.1
  419.1 3.4 copy-start.1
  444.5 77.1 %reduce-scatter.10.cloned.1.call-start = ((), (), s32[]{:S(2)}) async-start(), calls=%async_computation.6 | async-start | bytes 294912
Sparse Core Ops, SparseCore 0:
  33.5 128.0 reduce-scatter.7
  164.4 84.7 all-gather.1
  444.6 35.5 reduce-scatter.11
  482.5 39.0 reduce-scatter.9
